TPU v7x, 32 devices: a whole 2x2x4 slice. The times are simulated.
32 devices in a mesh: dp: 4 (over z), head: 8 (over y, x, core).
Axes of the slice: x: 2, y: 2, z: 4, core: 2. Of those that a mesh axis runs over, the one named last changes fastest.
Arguments:
- tokens: bfloat16 [6144, 1152], P('dp'), may hold values from -6 to 6
- seg_ids: int32 [4, 1536], P('dp'), may hold values from 0 to 2, as said below
- time_steps: int32 [12], P('dp'), may hold values from 0 to 999
- head_masks: int32 [12, 16], P('dp', 'head'), may hold values 0 or 1
- skip_masks: int32 [4, 1536], P('dp'), may hold values 0 or 1
- ada_weight: bfloat16 [1152, 6912], P(None, 'head'), may hold values from -0.1875 to 0.1875
- ada_bias: bfloat16 [6912], P('head'), may hold values from -3 to 3
- qkv_weight: bfloat16 [1152, 3, 1152], P(None, None, 'head'), may hold values from -0.1875 to 0.1875
- qv_bias: bfloat16 [2, 1152], P(None, 'head'), may hold values from -2 to 2
- proj_weight: bfloat16 [1152, 1152], P('head'), may hold values from -3 to 3
- proj_bias: bfloat16 [1152], replicated, may hold values from -2 to 2
- fc1_weight: bfloat16 [1152, 4608], P(None, 'head'), may hold values from -0.1875 to 0.1875
- fc1_bias: bfloat16 [4608], P('head'), may hold values from -2 to 2
- fc2_weight: bfloat16 [4608, 1152], P('head'), may hold values from -0.09375 to 0.09375
- fc2_bias: bfloat16 [1152], replicated, may hold values from -2 to 2
- out_cotangent: bfloat16 [6144, 1152], P('dp'), may hold values from -6 to 6
Outputs:
- layer_out: bfloat16 [6144, 1152], P(('dp', 'head'))
- input_grad: float32 [6144, 1152], P(('dp', 'head'))
- ada_weight_grad: float32 [1152, 6912], P(None, 'head')
- ada_bias_grad: float32 [6912], P('head')
- qkv_weight_grad: float32 [1152, 3, 1152], P(None, None, 'head')
- qv_bias_grad: float32 [2, 1152], P(None, 'head')
- proj_weight_grad: float32 [1152, 1152], P('head')
- proj_bias_grad: float32 [1152], replicated
- fc1_weight_grad: float32 [1152, 4608], P(None, 'head')
- fc1_bias_grad: float32 [4608], P('head')
- fc2_weight_grad: float32 [4608, 1152], P('head')
- fc2_bias_grad: float32 [1152], replicated
Inputs may be any that keep to these rules, and one draw needn't show every extreme that they name: `seg_ids`: each pack holds one image of 1024 tokens and two images of 256 tokens, each on neighbouring positions, in an order that the draw chooses for each pack; the image numbers 0, 1, 2 never fall along a pack.
All inputs are finite; a program needn't handle non-finite values. No bound on the sum of `head_masks` or of `skip_masks` on one device may be relied on, other than what follows from the above.
Results may differ from a plain program's by a relative error of at most 0.01255.
The roundings to bfloat16 on the way count: a program that leaves them out, or rounds other values in their place, can miss the bound.
Values may be sent and summed in bfloat16 or wider, within the bound.
A program may use at most 192 MiB of HBM per device.

v0:
```python
import math
import jax
import jax.numpy as jnp
from jax import lax
from jax.sharding import PartitionSpec as P

HEAD_DIM = 72
highest = lax.Precision.HIGHEST


def embed_steps(steps, model_width):
    half_width = model_width // 2
    freqs = jnp.exp(-math.log(10000.0) * jnp.arange(half_width, dtype=jnp.float32) / half_width)
    angles = steps.astype(jnp.float32)[:, None] * freqs[None, :]
    return jnp.concatenate([jnp.cos(angles), jnp.sin(angles)], axis=1)


def normalize(value):
    center = value - jnp.mean(value, axis=-1, keepdims=True)
    return center * lax.rsqrt(jnp.mean(center * center, axis=-1, keepdims=True) + 1e-06)


def norm_back(value, grad):
    return jax.vjp(normalize, value)[1](grad)[0]


def gelu_tanh(value):
    return jax.nn.gelu(value, approximate=True)


def per_token(select, table):
    return jnp.dot(select, table, precision=highest)


def item_sums(select, values):
    return jnp.einsum("sg,sd->gd", select, values, precision=highest)


def attend_forward(queries, key_rows, value_rows, segment, heads_here, score_scale, block_rows):
    length = queries.shape[0]
    q_heads = queries.reshape(length, heads_here, -1)
    k_heads = key_rows.reshape(length, heads_here, -1)
    v_heads = value_rows.reshape(length, heads_here, -1)

    def one_block(start):
        q_block = lax.dynamic_slice_in_dim(q_heads, start, block_rows, 0)
        seg_query = lax.dynamic_slice_in_dim(segment, start, block_rows, 0)
        scores = (
            jnp.einsum("qhe,khe->hqk", q_block, k_heads, preferred_element_type=jnp.float32)
            * score_scale
        )
        scores = jnp.where((seg_query[:, None] == segment[None, :])[None], scores, -1e30)
        row_peak = jnp.max(scores, axis=-1, keepdims=True)
        row_exp = jnp.exp(scores - row_peak)
        row_total = jnp.sum(row_exp, axis=-1, keepdims=True)
        prob_low = (row_exp / row_total).astype(jnp.bfloat16)
        out_block = jnp.einsum(
            "hqk,khe->qhe", prob_low, v_heads, preferred_element_type=jnp.float32
        )
        return (out_block.reshape(block_rows, -1), (row_peak + jnp.log(row_total))[..., 0])

    starts = jnp.arange(length // block_rows, dtype=jnp.int32) * block_rows
    out_blocks, log_totals = lax.map(one_block, starts)
    return (out_blocks.reshape(length, -1), log_totals)


def attend_backward(
    queries,
    key_rows,
    value_rows,
    grad_attn,
    segment,
    log_totals,
    heads_here,
    score_scale,
    block_rows,
):
    length = queries.shape[0]
    q_heads = queries.reshape(length, heads_here, -1)
    k_heads = key_rows.reshape(length, heads_here, -1)
    v_heads = value_rows.reshape(length, heads_here, -1)
    g_heads = grad_attn.reshape(length, heads_here, -1)

    def one_block(carry, inputs):
        start, lse_block = inputs
        grad_keys_acc, grad_values_acc = carry
        q_block = lax.dynamic_slice_in_dim(q_heads, start, block_rows, 0)
        g_block = lax.dynamic_slice_in_dim(g_heads, start, block_rows, 0)
        seg_query = lax.dynamic_slice_in_dim(segment, start, block_rows, 0)
        scores = (
            jnp.einsum("qhe,khe->hqk", q_block, k_heads, preferred_element_type=jnp.float32)
            * score_scale
        )
        scores = jnp.where((seg_query[:, None] == segment[None, :])[None], scores, -1e30)
        probs = jnp.exp(scores - lse_block[..., None])
        grad_probs = jnp.einsum(
            "qhe,khe->hqk", g_block, v_heads, preferred_element_type=jnp.float32
        )
        row_delta = jnp.sum(grad_probs * probs, axis=-1, keepdims=True)
        grad_scores = (probs * (grad_probs - row_delta)).astype(jnp.bfloat16)
        grad_query = (
            jnp.einsum("hqk,khe->qhe", grad_scores, k_heads, preferred_element_type=jnp.float32)
            * score_scale
        )
        grad_keys_acc = grad_keys_acc + jnp.einsum(
            "hqk,qhe->khe", grad_scores, q_block, preferred_element_type=jnp.float32
        )
        grad_values_acc = grad_values_acc + jnp.einsum(
            "hqk,qhe->khe", probs.astype(jnp.bfloat16), g_block, preferred_element_type=jnp.float32
        )
        return (
            (grad_keys_acc, grad_values_acc),
            grad_query.astype(jnp.bfloat16).reshape(block_rows, -1),
        )

    starts = jnp.arange(length // block_rows, dtype=jnp.int32) * block_rows
    zeros_acc = jnp.zeros(k_heads.shape, jnp.float32)
    (grad_keys_acc, grad_values_acc), grad_query = lax.scan(
        one_block, (zeros_acc, zeros_acc), (starts, log_totals)
    )
    grad_keys = (grad_keys_acc * score_scale).astype(jnp.bfloat16).reshape(length, -1)
    grad_values = grad_values_acc.astype(jnp.bfloat16).reshape(length, -1)
    return (grad_query.reshape(length, -1), grad_keys, grad_values)


def local(
    tokens,
    seg_ids,
    time_steps,
    head_masks,
    skip_masks,
    ada_weight,
    ada_bias,
    qkv_weight,
    qv_bias,
    proj_weight,
    proj_bias,
    fc1_weight,
    fc1_bias,
    fc2_weight,
    fc2_bias,
    out_cotangent,
):
    length, model_width = tokens.shape
    groups = time_steps.shape[0]
    heads_here = qkv_weight.shape[2] // HEAD_DIM
    score_scale = HEAD_DIM ** (-0.5)
    block_rows = min(512, length)
    share_rows = length // lax.axis_size("head")
    row_start = lax.axis_index("head") * share_rows
    segment = seg_ids[0]
    keep_tok = skip_masks[0].astype(jnp.float32)[:, None]
    select = (segment[:, None] == jnp.arange(groups, dtype=jnp.int32)[None, :]).astype(jnp.float32)

    def own_rows(value):
        return lax.dynamic_slice_in_dim(value, row_start, share_rows, 0)

    time_act = jax.nn.silu(embed_steps(time_steps, model_width)).astype(jnp.bfloat16)
    mod_part = jnp.dot(time_act, ada_weight, preferred_element_type=jnp.float32) + ada_bias.astype(
        jnp.float32
    )
    modulation = lax.all_gather(mod_part, "head", axis=1, tiled=True)
    shift_one, scale_one = [
        per_token(select, modulation[:, k * model_width : (k + 1) * model_width]) for k in (0, 1)
    ]
    x_full = tokens.astype(jnp.float32)
    norm_one = normalize(x_full)
    h_one = (norm_one * (1.0 + scale_one) + shift_one).astype(jnp.bfloat16)
    proj_three = jnp.einsum("sd,dcj->csj", h_one, qkv_weight, preferred_element_type=jnp.float32)
    qv_float = qv_bias.astype(jnp.float32)
    queries = (proj_three[0] + qv_float[0]).astype(jnp.bfloat16)
    key_rows = proj_three[1].astype(jnp.bfloat16)
    value_rows = (proj_three[2] + qv_float[1]).astype(jnp.bfloat16)
    attended, log_totals = attend_forward(
        queries, key_rows, value_rows, segment, heads_here, score_scale, block_rows
    )
    head_keep = jnp.repeat(per_token(select, head_masks.astype(jnp.float32)), HEAD_DIM, axis=1)
    attn_low = (attended * head_keep).astype(jnp.bfloat16)
    proj_b = proj_bias.astype(jnp.float32)
    fc1_b = fc1_bias.astype(jnp.float32)
    fc2_b = fc2_bias.astype(jnp.float32)

    def scatter_sum(part):
        return lax.psum_scatter(
            part.astype(jnp.bfloat16), "head", scatter_dimension=0, tiled=True
        ).astype(jnp.float32)

    def share_rows_of(value):
        return lax.all_gather(value, "head", axis=0, tiled=True)

    attn_part = jnp.dot(attn_low, proj_weight, preferred_element_type=jnp.float32)
    branch_a = scatter_sum(attn_part) + proj_b
    x_own = own_rows(tokens).astype(jnp.float32)
    select_own = own_rows(select)
    keep_own = own_rows(keep_tok)
    cot_own = own_rows(out_cotangent).astype(jnp.float32)
    shift_one_o, scale_one_o, gate_one_o, shift_two_o, scale_two_o, gate_two_o = jnp.split(
        per_token(select_own, modulation), 6, axis=1
    )
    mid_rows = x_own + gate_one_o * branch_a
    norm_two = normalize(mid_rows)
    h_two = share_rows_of((norm_two * (1.0 + scale_two_o) + shift_two_o).astype(jnp.bfloat16))
    hidden = jnp.dot(h_two, fc1_weight, preferred_element_type=jnp.float32) + fc1_b
    gelu_out = gelu_tanh(hidden).astype(jnp.bfloat16)
    mlp_part = jnp.dot(gelu_out, fc2_weight, preferred_element_type=jnp.float32)
    gate_two = per_token(select, modulation[:, 5 * model_width :])
    grad_m = (out_cotangent.astype(jnp.float32) * gate_two * keep_tok).astype(jnp.bfloat16)
    grad_gelu = jnp.einsum("sd,fd->sf", grad_m, fc2_weight, preferred_element_type=jnp.float32)
    grad_hidden = jax.vjp(gelu_tanh, hidden)[1](grad_gelu)[0].astype(jnp.bfloat16)
    h_two_part = jnp.einsum(
        "sf,df->sd", grad_hidden, fc1_weight, preferred_element_type=jnp.float32
    )
    grad_h_two = scatter_sum(h_two_part)
    fc2_grad = jnp.einsum("sf,sd->fd", gelu_out, grad_m, preferred_element_type=jnp.float32)
    fc2_bias_grad = jnp.sum(grad_m.astype(jnp.float32), axis=0)
    fc1_grad = jnp.einsum("sd,sf->df", h_two, grad_hidden, preferred_element_type=jnp.float32)
    fc1_bias_grad = jnp.sum(grad_hidden.astype(jnp.float32), axis=0)
    branch_m = scatter_sum(mlp_part) + fc2_b
    layer_out = (mid_rows + gate_two_o * keep_own * branch_m).astype(jnp.bfloat16)
    gate_two_grad = item_sums(select_own, cot_own * keep_own * branch_m)
    grad_mid = cot_own + norm_back(mid_rows, grad_h_two * (1.0 + scale_two_o))
    shift_two_grad = item_sums(select_own, grad_h_two)
    scale_two_grad = item_sums(select_own, grad_h_two * norm_two)
    gate_one_grad = item_sums(select_own, grad_mid * branch_a)
    grad_a = share_rows_of((grad_mid * gate_one_o).astype(jnp.bfloat16))
    proj_bias_grad = jnp.sum(grad_a.astype(jnp.float32), axis=0)
    proj_grad = jnp.einsum("sj,sd->jd", attn_low, grad_a, preferred_element_type=jnp.float32)
    grad_attn_low = jnp.einsum(
        "sd,jd->sj", grad_a, proj_weight, preferred_element_type=jnp.float32
    ).astype(jnp.bfloat16)
    grad_attn = grad_attn_low * head_keep.astype(jnp.bfloat16)
    grad_queries, grad_keys, grad_values = attend_backward(
        queries,
        key_rows,
        value_rows,
        grad_attn,
        segment,
        log_totals,
        heads_here,
        score_scale,
        block_rows,
    )
    grad_three = jnp.stack([grad_queries, grad_keys, grad_values])
    qkv_grad = jnp.einsum("sd,csj->dcj", h_one, grad_three, preferred_element_type=jnp.float32)
    qv_bias_grad = jnp.stack(
        [
            jnp.sum(grad_queries.astype(jnp.float32), axis=0),
            jnp.sum(grad_values.astype(jnp.float32), axis=0),
        ]
    )
    h_one_part = jnp.einsum(
        "csj,dcj->sd", grad_three, qkv_weight, preferred_element_type=jnp.float32
    )
    grad_h_one = scatter_sum(h_one_part)
    input_grad = grad_mid + norm_back(x_own, grad_h_one * (1.0 + scale_one_o))
    shift_one_grad = item_sums(select_own, grad_h_one)
    scale_one_grad = item_sums(select_own, grad_h_one * normalize(x_own))
    mod_grad = jnp.concatenate(
        [
            shift_one_grad,
            scale_one_grad,
            gate_one_grad,
            shift_two_grad,
            scale_two_grad,
            gate_two_grad,
        ],
        axis=1,
    )
    mod_cols = lax.psum_scatter(mod_grad, "head", scatter_dimension=1, tiled=True)
    all_cols = lax.all_gather(mod_cols, "dp", axis=0, tiled=True)
    all_act = lax.all_gather(time_act, "dp", axis=0, tiled=True)
    ada_grad = jnp.einsum("gd,gc->dc", all_act.astype(jnp.float32), all_cols, precision=highest)
    ada_bias_grad = jnp.sum(all_cols, axis=0)
    summed = lax.psum(
        (
            qkv_grad.astype(jnp.bfloat16),
            proj_grad.astype(jnp.bfloat16),
            fc1_grad.astype(jnp.bfloat16),
            fc2_grad.astype(jnp.bfloat16),
        ),
        "dp",
    )
    qkv_grad, proj_grad, fc1_grad, fc2_grad = [g.astype(jnp.float32) for g in summed]
    qv_bias_grad, proj_bias_grad, fc1_bias_grad, fc2_bias_grad = lax.psum(
        (qv_bias_grad, proj_bias_grad, fc1_bias_grad, fc2_bias_grad), "dp"
    )
    return (
        layer_out,
        input_grad,
        ada_grad,
        ada_bias_grad,
        qkv_grad,
        qv_bias_grad,
        proj_grad,
        proj_bias_grad,
        fc1_grad,
        fc1_bias_grad,
        fc2_grad,
        fc2_bias_grad,
    )


def solution(mesh):
    placed = (
        P("dp", None),
        P("dp", None),
        P("dp"),
        P("dp", "head"),
        P("dp", None),
        P(None, "head"),
        P("head"),
        P(None, None, "head"),
        P(None, "head"),
        P("head", None),
        P(),
        P(None, "head"),
        P("head"),
        P("head", None),
        P(),
        P("dp", None),
    )
    return jax.shard_map(
        local,
        mesh=mesh,
        in_specs=placed,
        out_specs=(
            P(("dp", "head"), None),
            P(("dp", "head"), None),
            P(None, "head"),
            P("head"),
            P(None, None, "head"),
            P(None, "head"),
            P("head", None),
            P(),
            P(None, "head"),
            P("head"),
            P("head", None),
            P(),
        ),
        check_vma=False,
    )
```

profile of v0, /device:TPU:0, one launch (start us, length us, event | category | flops | bytes accessed | tf_op | source)
XLA Modules:
  0.0 679.6 jit_solution(17424533891599629888)
XLA Ops:
  9.5 2.7 convert_reduce_fusion
  14.4 10.9 %all-gather = f32[8,864,3]{1,2,0:T(4,128)S(1)} all-gather(f32[1,864,3]{1,2,0:T(4,128)S(1)} %fusion.47), channel_id=1, replica_groups=mesh['dp'=4,'head'=8] {'head'}, dimensions={0}, use_global_device_ids=true | all-gather | bytes 93312 | tf_op jit(solution)/shard_map/all_gather | solution.py:162
  25.5 6.0 fusion.28
  31.5 3.7 fusion.33
  35.3 1.9 fusion.90
  40.1 43.2 %while.27 = (s32[]{:T(128)}, f32[3,512,144]{1,0,2:T(4,128)S(1)}, f32[3,2,512]{2,1,0:T(2,128)S(1)}, s32[3]{0:T(128)S(1)}, s32[1536]{0:T(1024)S(1)}, /*index=5*/s3...) while((s32[]{:T(128)}, f32[3,512,144]{1,0,2:T(4,128)S(1)}, ...), condition=%wide.region_5.6_spmd, body=%wide.region_2.5_spmd.sunk | while | flops 472644608 | bytes 24584384 | solution.py:63
  43.3 2.9 fusion.150
  46.1 2.0 fusion.151
  48.1 3.2 fusion.152
  51.7 2.8 dynamic_update_slice.19
  57.6 2.9 fusion.150
  60.5 2.0 fusion.151
  62.5 3.2 fusion.152
  66.0 2.8 dynamic_update_slice.19
  71.9 2.9 fusion.150
  74.8 2.0 fusion.151
  76.8 3.2 fusion.152
  80.3 2.8 dynamic_update_slice.19
  84.3 3.0 convolution_convert_fusion
  87.7 4.5 fusion.84
  92.3 43.7 %reduce-scatter.8.cloned.1.call-done = bf16[192,1152]{1,0:T(8,128)(2,1)} async-done(((bf16[1536,1152]{1,0:T(8,128)(2,1)}), bf16[192,1152]{1,0:T(8,128)(2,1)}) %reduce-scatter.8.cloned.1.call-update) | async-done | bytes 442384 | tf_op jit(solution)/shard_map/reduce_scatter | solution.py:184
  137.9 2.5 fusion.54
  140.5 6.0 convert_reduce_fusion.1
  148.3 4.3 fusion.91
  152.6 22.0 %all-gather.6.cloned.1.call-done = bf16[1536,1152]{1,0:T(8,128)(2,1)} async-done(((bf16[192,1152]{1,0:T(8,128)(2,1)}), bf16[1536,1152]{1,0:T(8,128)(2,1)}) %all-gather.6.cloned.1.call-update) | async-done | bytes 3538960 | tf_op jit(solution)/shard_map/all_gather | solution.py:189
  174.5 8.7 %convert_reduce_fusion.3 = (f32[576]{0:T(1024)S(1)}, bf16[1536,576]{0,1:T(8,128)(2,1)S(1)}, f32[1536,576]{0,1:T(8,128)}) fusion(f32[1536,576]{0,1:T(8,128)} %fusion.91, f32[576]{0:T(1024)S(1)} %convert_element_type.194, bf16[1536,1152]{1,0:T(8,128)(2,1)} %all-gather.6.cloned.1.call-done, bf16[1152,576]{0,1:T(8,128)(2,1)S(1)} %copy-done.33), kind=kOutput, calls=%fused_computation.64 | convolution fusion | flops 2058780160 | bytes 13718016 | tf_op jit(solution)/shard_map/dot_general | solution.py:203
  184.4 4.6 convolution_convert_fusion.1
  190.4 7.3 %convolution_convert_fusion.2 = bf16[1536,1152]{1,0:T(8,128)(2,1)} fusion(bf16[576,1152]{1,0:T(8,128)(2,1)S(1)} %copy-done.35, f32[1536,576]{0,1:T(8,128)} %get-tuple-element.244), kind=kOutput, calls=%fused_computation.50 | convolution fusion | flops 2048163840 | bytes 8404992 | tf_op jit(solution)/shard_map/dot_general | solution.py:205
  198.5 38.9 %reduce-scatter.12.cloned.1.call-done = bf16[192,1152]{1,0:T(8,128)(2,1)} async-done(((bf16[1536,1152]{1,0:T(8,128)(2,1)}), bf16[192,1152]{1,0:T(8,128)(2,1)}) %reduce-scatter.12.cloned.1.call-update) | async-done | bytes 442384 | tf_op jit(solution)/shard_map/reduce_scatter | solution.py:184
  238.9 49.9 %reduce-scatter.10.cloned.1.call-done = bf16[192,1152]{1,0:T(8,128)(2,1)} async-done(((bf16[1536,1152]{1,0:T(8,128)(2,1)}), bf16[192,1152]{1,0:T(8,128)(2,1)}) %reduce-scatter.10.cloned.1.call-update) | async-done | bytes 442384 | tf_op jit(solution)/shard_map/reduce_scatter | solution.py:184
  288.8 2.9 fusion.87
  291.7 2.6 multiply_convert_fusion.3
  294.4 6.2 convolution_convert_fusion.3
  300.7 4.2 convolution_convert_fusion.4
  304.8 23.6 %all-gather.8.cloned.1.call-done = bf16[1536,1152]{1,0:T(8,128)(2,1)} async-done(((bf16[192,1152]{1,0:T(8,128)(2,1)}), bf16[1536,1152]{1,0:T(8,128)(2,1)}) %all-gather.8.cloned.1.call-update) | async-done | bytes 3538960 | tf_op jit(solution)/shard_map/all_gather | solution.py:189
  328.4 4.1 fusion.42
  332.5 47.8 %while.28 = (s32[]{:T(128)}, f32[1536,2,72]{0,2,1:T(8,128)}, f32[1536,2,72]{0,2,1:T(8,128)S(1)}, bf16[3,512,144]{1,2,0:T(8,128)(2,1)}, s32[3]{0:T(128)S(1)}, /*i...) while((s32[]{:T(128)}, f32[1536,2,72]{0,2,1:T(8,128)}, ...), condition=%wide.region_15.16_spmd.clone, body=%wide.region_13.15_spmd.clone.sunk | while | flops 1148435456 | bytes 61780260 | solution.py:118
  335.8 3.1 subtract_exponential_fusion.3
  338.9 1.8 fusion.163
  340.7 2.4 multiply_reduce_fusion.4
  343.7 2.2 fusion.164
  351.7 3.1 subtract_exponential_fusion.3
  354.8 1.8 fusion.163
  356.6 2.4 multiply_reduce_fusion.4
  359.6 2.2 fusion.164
  367.6 3.1 subtract_exponential_fusion.3
  372.5 2.4 multiply_reduce_fusion.4
  375.5 2.2 fusion.164
  385.6 1.9 fusion.93
  391.2 4.0 fusion.31
  396.1 13.6 %all-gather.1 = bf16[4,3,1152]{2,1,0:T(4,128)(2,1)S(1)} all-gather(bf16[1,3,1152]{2,1,0:T(4,128)(2,1)S(1)} %fusion.129), channel_id=1, replica_groups=mesh['dp'=4,'head'=8] {'dp'}, dimensions={0}, use_global_device_ids=true | all-gather | bytes 34560 | tf_op jit(solution)/shard_map/all_gather | solution.py:271
  410.0 2.6 convert_reduce_fusion.2
  412.5 21.6 %all-reduce = (f32[2,144]{1,0:T(2,128)}, f32[1152]{0:T(1024)}, f32[576]{0:T(1024)}, f32[1152]{0:T(1024)}) all-reduce(f32[2,144]{1,0:T(2,128)S(1)} %pad_maximum_fusion.2, f32[1152]{0:T(1024)S(1)} %convert_reduce_fusion.2, f32[576]{0:T(1024)S(1)} %get-tuple-element.222, ...), channel_id=1, replica_groups=mesh['dp'=4,'head'=8] {'dp'}, use_global_device_ids=true, to_apply=%region_26.27 | all-reduce | flops 3168 | bytes 25344 | tf_op jit(solution)/shard_map/psum | solution.py:284
  434.2 106.8 %all-reduce.4.cloned.1.call-done = (bf16[1152,3,144]{0,2,1:T(8,128)(2,1)}, bf16[144,1152]{1,0:T(8,128)(2,1)}, bf16[1152,576]{0,1:T(8,128)(2,1)}, bf16[576,1152]{1,0:T(8,128)(2,1)}) async-done(((bf16[1152,3,144]{0,2,1:T(8,128)(2,1)}, bf16[144,1152]{1,0:T(8,128)(2,1)}, bf16[1152,576]{0,1:T(8,128)(2,1)}, bf16[576,1152]{1,0:T(8,128)(2,1)}), (bf16[1152,3,144]{0,2,1:T(8,128)(2,1)}, bf16[144,1152]{1,0:T(8,128)(2,1)}, ...) | async-done | bytes 3981328 | tf_op jit(solution)/shard_map/psum | solution.py:274
  541.0 2.0 convert_element_type.219
  543.0 2.7 convert_element_type.215
  549.1 43.5 %reduce-scatter.14.cloned.1.call-done = bf16[192,1152]{1,0:T(8,128)(2,1)} async-done(((bf16[1536,1152]{1,0:T(8,128)(2,1)}), bf16[192,1152]{1,0:T(8,128)(2,1)}) %reduce-scatter.14.cloned.1.call-update) | async-done | bytes 442384 | tf_op jit(solution)/shard_map/reduce_scatter | solution.py:184
  592.6 1.9 fusion.50
  594.5 2.7 fusion.86
  603.3 2.4 copy.36
  605.7 2.6 add_add_fusion.2
  608.3 45.6 %reduce-scatter.16.cloned.1.call-done = f32[864,3]{1,0:T(8,128)} async-done(((f32[6912,3]{1,0:T(8,128)}), f32[864,3]{1,0:T(8,128)}) %reduce-scatter.16.cloned.1.call-update) | async-done | bytes 10384
  655.1 13.1 %all-gather.2 = f32[4,3,864]{2,1,0:T(4,128)S(1)} all-gather(f32[1,3,864]{2,1,0:T(4,128)S(1)} %bitcast.149), channel_id=1, replica_groups=mesh['dp'=4,'head'=8] {'dp'}, dimensions={0}, use_global_device_ids=true | all-gather | bytes 51840 | tf_op jit(solution)/shard_map/all_gather | solution.py:270
  668.9 3.7 fusion.92
  (221 shorter events, 58.7 us)
Async XLA Ops:
  7.2 6.6 copy-start
  7.2 128.7 %reduce-scatter.8.cloned.1.call-start = ((), (), s32[]{:S(2)}) async-start(), calls=%async_computation.5 | async-start | bytes 3981312 | tf_op jit(solution)/shard_map/reduce_scatter | solution.py:184
  9.5 3.1 copy-start.2
  13.8 17.7 %copy-start.24 = (f32[3,576]{1,0:T(4,128)}, f32[3,576]{1,0:T(4,128)S(1)}, u32[]{:S(2)}) copy-start(f32[3,576]{1,0:T(4,128)S(1)} %get-tuple-element.240) | copy-start | bytes 20740
  13.8 17.7 %copy-start.26 = (f32[3,576]{1,0:T(4,128)}, f32[3,576]{1,0:T(4,128)S(1)}, u32[]{:S(2)}) copy-start(f32[3,576]{1,0:T(4,128)S(1)} %get-tuple-element.241) | copy-start | bytes 20740
  31.5 3.8 copy-start.36
  35.3 2.0 copy-start.12
  37.2 1.0 copy-start.32
  37.3 1.2 copy-start.38
  37.3 2.9 copy-start.18
  83.3 1.0 copy-start.22
  84.3 3.1 copy-start.9
  84.3 3.1 copy-start.29
  87.4 87.2 %all-gather.6.cloned.1.call-start = ((), (), s32[]{:S(2)}) async-start(), calls=%async_computation.6 | async-start | bytes 3981312 | tf_op jit(solution)/shard_map/all_gather | solution.py:189
  87.7 4.5 copy-start.19
  92.3 48.2 %copy-start.31 = (bf16[576]{0:T(1024)(128)(2,1)S(1)}, bf16[576]{0:T(1024)(128)(2,1)}, u32[]{:S(2)}) copy-start(bf16[576]{0:T(1024)(128)(2,1)} %param.32) | copy-start | bytes 3460
  92.3 48.2 %copy-start.28 = (s32[1,1536]{1,0:T(1,128)S(1)}, s32[1,1536]{1,0:T(1,128)}, u32[]{:S(2)}) copy-start(s32[1,1536]{1,0:T(1,128)} %param.24) | copy-start | bytes 18436
  140.4 96.9 %reduce-scatter.12.cloned.1.call-start = ((), (), s32[]{:S(2)}) async-start(), calls=%async_computation.8 | async-start | bytes 3981312 | tf_op jit(solution)/shard_map/reduce_scatter | solution.py:184
  140.5 7.8 %copy-start.34 = (bf16[576,1152]{1,0:T(8,128)(2,1)S(1)}, bf16[576,1152]{1,0:T(8,128)(2,1)}, u32[]{:S(2)}) copy-start(bf16[576,1152]{1,0:T(8,128)(2,1)} %param.33) | copy-start | bytes 3981316
  146.5 1.8 copy-start.39
  148.3 26.2 %copy-start.33 = (bf16[1152,576]{0,1:T(8,128)(2,1)S(1)}, bf16[1152,576]{0,1:T(8,128)(2,1)}, u32[]{:S(2)}) copy-start(bf16[1152,576]{0,1:T(8,128)(2,1)} %param.31) | copy-start | bytes 3981316
  183.2 1.2 copy-start.42
  189.1 1.3 copy-start.35
  189.1 99.7 %reduce-scatter.10.cloned.1.call-start = ((), (), s32[]{:S(2)}) async-start(), calls=%async_computation.7 | async-start | bytes 3981312 | tf_op jit(solution)/shard_map/reduce_scatter | solution.py:184
  197.7 0.7 copy-start.30
  197.7 130.7 %all-gather.8.cloned.1.call-start = ((), (), s32[]{:S(2)}) async-start(), calls=%async_computation.9 | async-start | bytes 3981312 | tf_op jit(solution)/shard_map/all_gather | solution.py:189
  291.7 2.7 copy-start.6
  294.3 246.7 %all-reduce.4.cloned.1.call-start = ((), (), s32[]{:S(2)}) async-start(), calls=%async_computation.12 | async-start | bytes 7962624 | tf_op jit(solution)/shard_map/psum | solution.py:274
  294.4 6.2 copy-start.40
  294.4 6.2 copy-start.41
  300.6 27.8 %copy-start.23 = (bf16[144,1152]{1,0:T(8,128)(2,1)S(1)}, bf16[144,1152]{1,0:T(8,128)(2,1)}, u32[]{:S(2)}) copy-start(bf16[144,1152]{1,0:T(8,128)(2,1)} %param.29) | copy-start | bytes 995332
  343.7 2.2 copy-start.3
  347.6 1.0 copy-start.4
  359.6 2.2 copy-start.3
  363.5 1.0 copy-start.4
  375.4 2.2 copy-start.3
  379.4 1.0 copy-start.4
  383.6 2.0 copy-start.13
  385.6 2.9 copy-start.5
  385.6 2.9 copy-start.10
  390.0 1.2 copy-start.37
  390.0 202.5 %reduce-scatter.14.cloned.1.call-start = ((), (), s32[]{:S(2)}) async-start(), calls=%async_computation.10 | async-start | bytes 3981312 | tf_op jit(solution)/shard_map/reduce_scatter | solution.py:184
  395.3 0.7 copy-start.25
  395.3 0.7 copy-start.27
  395.3 14.5 %copy-start.15 = (bf16[3,512,144]{1,2,0:T(8,128)(2,1)S(1)}, bf16[3,512,144]{1,2,0:T(8,128)(2,1)}, u32[]{:S(2)}) copy-start(bf16[3,512,144]{1,2,0:T(8,128)(2,1)} %get-tuple-element.126) | copy-start | bytes 1327108
  395.3 258.6 %reduce-scatter.16.cloned.1.call-start = ((), (), s32[]{:S(2)}) async-start(), calls=%async_computation.11 | async-start | bytes 3981312
  541.0 4.7 copy-start.17
  543.0 4.4 copy-start.16
  547.4 49.8 %copy-start.20 = (pred[1536,3]{1,0:T(32,128)(4,1)S(1)}, pred[1536,3]{1,0:T(32,128)(4,1)}, u32[]{:S(2)}) copy-start(pred[1536,3]{1,0:T(32,128)(4,1)} %copy-done.19) | copy-start | bytes 13828
  549.1 50.0 %copy-start.7 = (f32[192,1152]{1,0:T(8,128)S(1)}, f32[192,1152]{1,0:T(8,128)}, u32[]{:S(2)}) copy-start(f32[192,1152]{1,0:T(8,128)} %copy-done.6) | copy-start | bytes 2654212
  549.1 50.0 %copy-start.14 = (bf16[192,1152]{1,0:T(8,128)(2,1)S(1)}, bf16[192,1152]{1,0:T(8,128)(2,1)}, u32[]{:S(2)}) copy-start(bf16[192,1152]{1,0:T(8,128)(2,1)} %reduce-scatter.8.cloned.1.call-done) | copy-start | bytes 1327108
  549.1 51.7 %copy-start.8 = (bf16[192,1152]{1,0:T(8,128)(2,1)S(1)}, bf16[192,1152]{1,0:T(8,128)(2,1)}, u32[]{:S(2)}) copy-start(bf16[192,1152]{1,0:T(8,128)(2,1)} %reduce-scatter.12.cloned.1.call-done) | copy-start | bytes 1327108
  592.6 4.6 copy-start.11
  594.5 7.2 %copy-start.21 = (bf16[192,1152]{1,0:T(8,128)(2,1)S(1)}, bf16[192,1152]{1,0:T(8,128)(2,1)}, u32[]{:S(2)}) copy-start(bf16[192,1152]{1,0:T(8,128)(2,1)} %reduce-scatter.10.cloned.1.call-done) | copy-start | bytes 1327108
  605.7 66.9 %copy-start.1 = (bf16[1152,864]{0,1:T(8,128)(2,1)S(1)}, bf16[1152,864]{0,1:T(8,128)(2,1)}, u32[]{:S(2)}) copy-start(bf16[1152,864]{0,1:T(8,128)(2,1)} %param.25) | copy-start | bytes 5971972
Sparse Core Ops, SparseCore 0:
  87.5 48.3 reduce-scatter.7
  140.5 33.9 all-gather.5
  189.2 48.0 reduce-scatter.11
  240.7 48.0 reduce-scatter.9
  294.4 33.9 all-gather.7
  390.2 150.7 all-reduce.3
  545.5 47.0 reduce-scatter.13
  605.8 48.0 reduce-scatter.15
where the time goes:
time: 684 us; the launch traced here: 680 us
  waiting for transfers between devices  374 us (55%)
  matrix products  135 us (20%)
  blocking collectives  59.2 us (9%)
  other arithmetic  51.4 us (8%)
  local copies, waits for them, and re-layouts  32.4 us (5%)
  between operations  14.9 us (2%)
  loops' own time  12.4 us (2%)
    reduce_scatter x4, waiting for transfers between devices, scatter_sum(): lax.psum_scatter(part.astype(jnp.bfloat16), 'head', scatter_dimension=0,...  176 us
    psum x1, waiting for transfers between devices, local(): lax.psum((qkv_grad.astype(jnp.bfloat16), proj_grad.astype(jnp.bfloat16),...  107 us
    unnamed x9, waiting for transfers between devices  45.7 us
    all_gather x2, waiting for transfers between devices, share_rows_of(): return lax.all_gather(value, 'head', axis=0, tiled=True)  45.5 us
    psum x1, blocking collectives, local(): lax.psum((qv_bias_grad, proj_bias_grad, fc1_bias_grad, fc2_bias_grad), 'dp')  21.6 us
    dot_general x5, matrix products, per_token(): return jnp.dot(select, table, precision=highest)  20.8 us
    dot_general x6, matrix products, one_block(): jnp.einsum('qhe,khe->hqk', q_block, k_heads, preferred_element_type=jnp.f...  17.9 us
  transfers between devices with their start and end apart: 8, of which 8 were waited for; matrix products, arithmetic and copies ran while one was open for 8% of the time, Pallas kernels for 0%

commit v1 on v0

--- a/solution.py
+++ b/solution.py
@@ -267,8 +267,11 @@
         axis=1,
     )
     mod_cols = lax.psum_scatter(mod_grad, "head", scatter_dimension=1, tiled=True)
-    all_cols = lax.all_gather(mod_cols, "dp", axis=0, tiled=True)
-    all_act = lax.all_gather(time_act, "dp", axis=0, tiled=True)
+    all_cols, all_act = jnp.split(
+        lax.all_gather(jnp.concatenate([mod_cols, time_act], axis=1), "dp", axis=0, tiled=True),
+        [mod_cols.shape[1]],
+        axis=1,
+    )
     ada_grad = jnp.einsum("gd,gc->dc", all_act.astype(jnp.float32), all_cols, precision=highest)
     ada_bias_grad = jnp.sum(all_cols, axis=0)
     summed = lax.psum(

time: 684 us -> 685 us (level)
  blocking collectives: 59.2 us -> 45 us
  waiting for transfers between devices: 374 us -> 388 us
    psum x1, waiting for transfers between devices: 107 us -> 121 us  [local(): lax.psum((qkv_grad.astype(jnp.bfloat16), proj_grad.astype(jnp.bfloat16),...]
    all_gather x2 -> x1, blocking collectives: 26.7 us -> 13.5 us  [local(): lax.all_gather(jnp.concatenate([mod_cols, time_act], axis=1), 'dp', axis=...]
where the time goes in v1:
time: 685 us; the launch traced here: 681 us
  waiting for transfers between devices  388 us (57%)
  matrix products  136 us (20%)
  other arithmetic  51.5 us (8%)
  blocking collectives  45 us (7%)
  local copies, waits for them, and re-layouts  32.5 us (5%)
  between operations  14.9 us (2%)
  loops' own time  12.4 us (2%)
    reduce_scatter x4, waiting for transfers between devices, scatter_sum(): lax.psum_scatter(part.astype(jnp.bfloat16), 'head', scatter_dimension=0,...  176 us
    psum x1, waiting for transfers between devices, local(): lax.psum((qkv_grad.astype(jnp.bfloat16), proj_grad.astype(jnp.bfloat16),...  121 us
    unnamed x9, waiting for transfers between devices  45.7 us
    all_gather x2, waiting for transfers between devices, share_rows_of(): return lax.all_gather(value, 'head', axis=0, tiled=True)  45.5 us
    dot_general x5, matrix products, per_token(): return jnp.dot(select, table, precision=highest)  20.8 us
    psum x1, blocking collectives, local(): lax.psum((qv_bias_grad, proj_bias_grad, fc1_bias_grad, fc2_bias_grad), 'dp')  20.7 us
    dot_general x6, matrix products, one_block(): jnp.einsum('qhe,khe->hqk', q_block, k_heads, preferred_element_type=jnp.f...  17.9 us
  transfers between devices with their start and end apart: 8, of which 8 were waited for; matrix products, arithmetic and copies ran while one was open for 8% of the time, Pallas kernels for 0%

profile of v1, /device:TPU:0, one launch (start us, length us, event | category | flops | bytes accessed | tf_op | source)
XLA Modules:
  0.0 681.1 jit_solution(15921227245692752176)
XLA Ops:
  9.5 2.7 convert_reduce_fusion
  14.4 10.9 %all-gather = f32[8,864,3]{1,2,0:T(4,128)S(1)} all-gather(f32[1,864,3]{1,2,0:T(4,128)S(1)} %fusion.47), channel_id=1, replica_groups=mesh['dp'=4,'head'=8] {'head'}, dimensions={0}, use_global_device_ids=true | all-gather | bytes 93312 | tf_op jit(solution)/shard_map/all_gather | solution.py:162
  25.5 6.0 fusion.28
  31.5 3.7 fusion.33
  35.3 1.9 fusion.95
  40.1 43.2 %while.27 = (s32[]{:T(128)}, f32[3,512,144]{1,0,2:T(4,128)S(1)}, f32[3,2,512]{2,1,0:T(2,128)S(1)}, s32[3]{0:T(128)S(1)}, s32[1536]{0:T(1024)S(1)}, /*index=5*/s3...) while((s32[]{:T(128)}, f32[3,512,144]{1,0,2:T(4,128)S(1)}, ...), condition=%wide.region_5.6_spmd, body=%wide.region_2.5_spmd.sunk | while | flops 472644608 | bytes 24584384 | solution.py:63
  43.3 2.9 fusion.149
  46.1 2.0 fusion.150
  48.1 3.2 fusion.151
  51.7 2.8 dynamic_update_slice.19
  57.6 2.9 fusion.149
  60.5 2.0 fusion.150
  62.5 3.2 fusion.151
  66.0 2.8 dynamic_update_slice.19
  71.9 2.9 fusion.149
  74.8 2.0 fusion.150
  76.8 3.2 fusion.151
  80.3 2.8 dynamic_update_slice.19
  84.3 3.0 convolution_convert_fusion
  87.7 4.5 fusion.89
  92.3 43.7 %reduce-scatter.8.cloned.1.call-done = bf16[192,1152]{1,0:T(8,128)(2,1)} async-done(((bf16[1536,1152]{1,0:T(8,128)(2,1)}), bf16[192,1152]{1,0:T(8,128)(2,1)}) %reduce-scatter.8.cloned.1.call-update) | async-done | bytes 442384 | tf_op jit(solution)/shard_map/reduce_scatter | solution.py:184
  137.9 2.5 fusion.54
  140.5 6.0 convert_reduce_fusion.1
  146.5 1.8 copy-done.39
  148.3 4.3 fusion.96
  152.6 22.0 %all-gather.5.cloned.1.call-done = bf16[1536,1152]{1,0:T(8,128)(2,1)} async-done(((bf16[192,1152]{1,0:T(8,128)(2,1)}), bf16[1536,1152]{1,0:T(8,128)(2,1)}) %all-gather.5.cloned.1.call-update) | async-done | bytes 3538960 | tf_op jit(solution)/shard_map/all_gather | solution.py:189
  174.5 8.7 %convert_reduce_fusion.3 = (f32[576]{0:T(1024)S(1)}, bf16[1536,576]{0,1:T(8,128)(2,1)S(1)}, f32[1536,576]{0,1:T(8,128)}) fusion(f32[1536,576]{0,1:T(8,128)} %fusion.96, f32[576]{0:T(1024)S(1)} %convert_element_type.196, bf16[1536,1152]{1,0:T(8,128)(2,1)} %all-gather.5.cloned.1.call-done, bf16[1152,576]{0,1:T(8,128)(2,1)S(1)} %copy-done.33), kind=kOutput, calls=%fused_computation.64 | convolution fusion | flops 2058780160 | bytes 13718016 | tf_op jit(solution)/shard_map/dot_general | solution.py:203
  184.4 4.6 convolution_convert_fusion.1
  190.4 7.3 %convolution_convert_fusion.2 = bf16[1536,1152]{1,0:T(8,128)(2,1)} fusion(bf16[576,1152]{1,0:T(8,128)(2,1)S(1)} %copy-done.35, f32[1536,576]{0,1:T(8,128)} %get-tuple-element.244), kind=kOutput, calls=%fused_computation.50 | convolution fusion | flops 2048163840 | bytes 8404992 | tf_op jit(solution)/shard_map/dot_general | solution.py:205
  198.5 38.9 %reduce-scatter.12.cloned.1.call-done = bf16[192,1152]{1,0:T(8,128)(2,1)} async-done(((bf16[1536,1152]{1,0:T(8,128)(2,1)}), bf16[192,1152]{1,0:T(8,128)(2,1)}) %reduce-scatter.12.cloned.1.call-update) | async-done | bytes 442384 | tf_op jit(solution)/shard_map/reduce_scatter | solution.py:184
  238.9 49.9 %reduce-scatter.10.cloned.1.call-done = bf16[192,1152]{1,0:T(8,128)(2,1)} async-done(((bf16[1536,1152]{1,0:T(8,128)(2,1)}), bf16[192,1152]{1,0:T(8,128)(2,1)}) %reduce-scatter.10.cloned.1.call-update) | async-done | bytes 442384 | tf_op jit(solution)/shard_map/reduce_scatter | solution.py:184
  288.8 2.9 fusion.92
  291.7 2.6 multiply_convert_fusion.3
  294.4 6.2 convolution_convert_fusion.3
  300.7 4.2 convolution_convert_fusion.4
  304.8 23.6 %all-gather.7.cloned.1.call-done = bf16[1536,1152]{1,0:T(8,128)(2,1)} async-done(((bf16[192,1152]{1,0:T(8,128)(2,1)}), bf16[1536,1152]{1,0:T(8,128)(2,1)}) %all-gather.7.cloned.1.call-update) | async-done | bytes 3538960 | tf_op jit(solution)/shard_map/all_gather | solution.py:189
  328.4 4.1 fusion.42
  332.5 47.8 %while.28 = (s32[]{:T(128)}, f32[1536,2,72]{0,2,1:T(8,128)}, f32[1536,2,72]{0,2,1:T(8,128)S(1)}, bf16[3,512,144]{1,2,0:T(8,128)(2,1)}, s32[3]{0:T(128)S(1)}, /*i...) while((s32[]{:T(128)}, f32[1536,2,72]{0,2,1:T(8,128)}, ...), condition=%wide.region_15.16_spmd.clone, body=%wide.region_13.15_spmd.clone.sunk | while | flops 1148435456 | bytes 61780260 | solution.py:118
  335.8 3.1 subtract_exponential_fusion.3
  338.9 1.8 fusion.162
  340.7 2.4 multiply_reduce_fusion.4
  343.7 2.2 fusion.163
  351.7 3.1 subtract_exponential_fusion.3
  354.8 1.8 fusion.162
  356.6 2.4 multiply_reduce_fusion.4
  359.6 2.2 fusion.163
  367.6 3.1 subtract_exponential_fusion.3
  372.5 2.4 multiply_reduce_fusion.4
  375.5 2.2 fusion.163
  385.6 1.9 fusion.97
  391.2 4.0 fusion.31
  396.6 2.6 convert_reduce_fusion.2
  399.2 20.7 %all-reduce = (f32[2,144]{1,0:T(2,128)}, f32[1152]{0:T(1024)}, f32[576]{0:T(1024)}, f32[1152]{0:T(1024)}) all-reduce(f32[2,144]{1,0:T(2,128)S(1)} %pad_maximum_fusion.2, f32[1152]{0:T(1024)S(1)} %convert_reduce_fusion.2, f32[576]{0:T(1024)S(1)} %get-tuple-element.222, ...), channel_id=1, replica_groups=mesh['dp'=4,'head'=8] {'dp'}, use_global_device_ids=true, to_apply=%region_26.27 | all-reduce | flops 3168 | bytes 25344 | tf_op jit(solution)/shard_map/psum | solution.py:287
  419.9 120.6 %all-reduce.4.cloned.1.call-done = (bf16[1152,3,144]{0,2,1:T(8,128)(2,1)}, bf16[144,1152]{1,0:T(8,128)(2,1)}, bf16[1152,576]{0,1:T(8,128)(2,1)}, bf16[576,1152]{1,0:T(8,128)(2,1)}) async-done(((bf16[1152,3,144]{0,2,1:T(8,128)(2,1)}, bf16[144,1152]{1,0:T(8,128)(2,1)}, bf16[1152,576]{0,1:T(8,128)(2,1)}, bf16[576,1152]{1,0:T(8,128)(2,1)}), (bf16[1152,3,144]{0,2,1:T(8,128)(2,1)}, bf16[144,1152]{1,0:T(8,128)(2,1)}, ...) | async-done | bytes 3981328 | tf_op jit(solution)/shard_map/psum | solution.py:277
  540.4 2.0 convert_element_type.222
  542.4 2.7 convert_element_type.218
  548.5 43.5 %reduce-scatter.14.cloned.1.call-done = bf16[192,1152]{1,0:T(8,128)(2,1)} async-done(((bf16[1536,1152]{1,0:T(8,128)(2,1)}), bf16[192,1152]{1,0:T(8,128)(2,1)}) %reduce-scatter.14.cloned.1.call-update) | async-done | bytes 442384 | tf_op jit(solution)/shard_map/reduce_scatter | solution.py:184
  592.0 1.9 fusion.50
  593.9 2.7 fusion.91
  602.7 2.4 copy.36
  605.1 2.6 add_add_fusion.2
  607.7 45.6 %reduce-scatter.16.cloned.1.call-done = f32[864,3]{1,0:T(8,128)} async-done(((f32[6912,3]{1,0:T(8,128)}), f32[864,3]{1,0:T(8,128)}) %reduce-scatter.16.cloned.1.call-update) | async-done | bytes 10384
  654.6 13.5 %all-gather.1 = f32[4,3,2016]{2,1,0:T(4,128)S(1)} all-gather(f32[1,3,2016]{2,1,0:T(4,128)S(1)} %maximum_bitcast_fusion), channel_id=1, replica_groups=mesh['dp'=4,'head'=8] {'dp'}, dimensions={0}, use_global_device_ids=true | all-gather | bytes 120960 | tf_op jit(solution)/shard_map/all_gather | solution.py:271
  668.8 5.3 fusion.75
  (220 shorter events, 57.3 us)
Async XLA Ops:
  7.2 6.6 copy-start
  7.2 128.7 %reduce-scatter.8.cloned.1.call-start = ((), (), s32[]{:S(2)}) async-start(), calls=%async_computation.5 | async-start | bytes 3981312 | tf_op jit(solution)/shard_map/reduce_scatter | solution.py:184
  9.5 3.1 copy-start.2
  13.8 17.7 %copy-start.24 = (f32[3,576]{1,0:T(4,128)}, f32[3,576]{1,0:T(4,128)S(1)}, u32[]{:S(2)}) copy-start(f32[3,576]{1,0:T(4,128)S(1)} %get-tuple-element.240) | copy-start | bytes 20740
  13.8 17.7 %copy-start.26 = (f32[3,576]{1,0:T(4,128)}, f32[3,576]{1,0:T(4,128)S(1)}, u32[]{:S(2)}) copy-start(f32[3,576]{1,0:T(4,128)S(1)} %get-tuple-element.241) | copy-start | bytes 20740
  31.5 3.8 copy-start.36
  35.3 2.0 copy-start.12
  37.2 1.0 copy-start.32
  37.3 1.2 copy-start.38
  37.3 2.9 copy-start.18
  83.3 1.0 copy-start.22
  84.3 3.1 copy-start.9
  84.3 3.1 copy-start.29
  87.4 87.2 %all-gather.5.cloned.1.call-start = ((), (), s32[]{:S(2)}) async-start(), calls=%async_computation.6 | async-start | bytes 3981312 | tf_op jit(solution)/shard_map/all_gather | solution.py:189
  87.7 4.5 copy-start.19
  92.3 48.2 %copy-start.31 = (bf16[576]{0:T(1024)(128)(2,1)S(1)}, bf16[576]{0:T(1024)(128)(2,1)}, u32[]{:S(2)}) copy-start(bf16[576]{0:T(1024)(128)(2,1)} %param.32) | copy-start | bytes 3460
  92.3 48.2 %copy-start.28 = (s32[1,1536]{1,0:T(1,128)S(1)}, s32[1,1536]{1,0:T(1,128)}, u32[]{:S(2)}) copy-start(s32[1,1536]{1,0:T(1,128)} %param.24) | copy-start | bytes 18436
  140.4 96.9 %reduce-scatter.12.cloned.1.call-start = ((), (), s32[]{:S(2)}) async-start(), calls=%async_computation.8 | async-start | bytes 3981312 | tf_op jit(solution)/shard_map/reduce_scatter | solution.py:184
  140.5 7.8 %copy-start.34 = (bf16[576,1152]{1,0:T(8,128)(2,1)S(1)}, bf16[576,1152]{1,0:T(8,128)(2,1)}, u32[]{:S(2)}) copy-start(bf16[576,1152]{1,0:T(8,128)(2,1)} %param.33) | copy-start | bytes 3981316
  146.5 1.8 copy-start.39
  148.3 26.2 %copy-start.33 = (bf16[1152,576]{0,1:T(8,128)(2,1)S(1)}, bf16[1152,576]{0,1:T(8,128)(2,1)}, u32[]{:S(2)}) copy-start(bf16[1152,576]{0,1:T(8,128)(2,1)} %param.31) | copy-start | bytes 3981316
  183.2 1.2 copy-start.42
  189.1 1.3 copy-start.35
  189.1 99.7 %reduce-scatter.10.cloned.1.call-start = ((), (), s32[]{:S(2)}) async-start(), calls=%async_computation.7 | async-start | bytes 3981312 | tf_op jit(solution)/shard_map/reduce_scatter | solution.py:184
  197.7 0.7 copy-start.30
  197.7 130.7 %all-gather.7.cloned.1.call-start = ((), (), s32[]{:S(2)}) async-start(), calls=%async_computation.9 | async-start | bytes 3981312 | tf_op jit(solution)/shard_map/all_gather | solution.py:189
  291.7 2.7 copy-start.6
  294.3 246.1 %all-reduce.4.cloned.1.call-start = ((), (), s32[]{:S(2)}) async-start(), calls=%async_computation.12 | async-start | bytes 7962624 | tf_op jit(solution)/shard_map/psum | solution.py:277
  294.4 6.2 copy-start.40
  294.4 6.2 copy-start.41
  300.6 27.8 %copy-start.23 = (bf16[144,1152]{1,0:T(8,128)(2,1)S(1)}, bf16[144,1152]{1,0:T(8,128)(2,1)}, u32[]{:S(2)}) copy-start(bf16[144,1152]{1,0:T(8,128)(2,1)} %param.29) | copy-start | bytes 995332
  343.7 2.2 copy-start.3
  347.6 1.0 copy-start.4
  359.6 2.2 copy-start.3
  363.5 1.0 copy-start.4
  375.4 2.2 copy-start.3
  379.4 1.0 copy-start.4
  383.6 2.0 copy-start.13
  385.6 2.9 copy-start.5
  385.6 2.9 copy-start.10
  390.0 1.2 copy-start.37
  390.0 202.0 %reduce-scatter.14.cloned.1.call-start = ((), (), s32[]{:S(2)}) async-start(), calls=%async_computation.10 | async-start | bytes 3981312 | tf_op jit(solution)/shard_map/reduce_scatter | solution.py:184
  395.3 0.7 copy-start.25
  395.3 0.7 copy-start.27
  395.3 1.2 copy-start.15
  395.3 258.0 %reduce-scatter.16.cloned.1.call-start = ((), (), s32[]{:S(2)}) async-start(), calls=%async_computation.11 | async-start | bytes 3981312
  540.4 4.7 copy-start.17
  542.4 4.4 copy-start.16
  546.8 49.8 %copy-start.20 = (pred[1536,3]{1,0:T(32,128)(4,1)S(1)}, pred[1536,3]{1,0:T(32,128)(4,1)}, u32[]{:S(2)}) copy-start(pred[1536,3]{1,0:T(32,128)(4,1)} %copy-done.19) | copy-start | bytes 13828
  548.5 50.0 %copy-start.7 = (f32[192,1152]{1,0:T(8,128)S(1)}, f32[192,1152]{1,0:T(8,128)}, u32[]{:S(2)}) copy-start(f32[192,1152]{1,0:T(8,128)} %copy-done.6) | copy-start | bytes 2654212
  548.5 50.0 %copy-start.14 = (bf16[192,1152]{1,0:T(8,128)(2,1)S(1)}, bf16[192,1152]{1,0:T(8,128)(2,1)}, u32[]{:S(2)}) copy-start(bf16[192,1152]{1,0:T(8,128)(2,1)} %reduce-scatter.8.cloned.1.call-done) | copy-start | bytes 1327108
  548.5 51.7 %copy-start.8 = (bf16[192,1152]{1,0:T(8,128)(2,1)S(1)}, bf16[192,1152]{1,0:T(8,128)(2,1)}, u32[]{:S(2)}) copy-start(bf16[192,1152]{1,0:T(8,128)(2,1)} %reduce-scatter.12.cloned.1.call-done) | copy-start | bytes 1327108
  592.0 4.6 copy-start.11
  593.9 7.2 %copy-start.21 = (bf16[192,1152]{1,0:T(8,128)(2,1)S(1)}, bf16[192,1152]{1,0:T(8,128)(2,1)}, u32[]{:S(2)}) copy-start(bf16[192,1152]{1,0:T(8,128)(2,1)} %reduce-scatter.10.cloned.1.call-done) | copy-start | bytes 1327108
  605.1 68.9 %copy-start.1 = (bf16[1152,864]{0,1:T(8,128)(2,1)S(1)}, bf16[1152,864]{0,1:T(8,128)(2,1)}, u32[]{:S(2)}) copy-start(bf16[1152,864]{0,1:T(8,128)(2,1)} %param.25) | copy-start | bytes 5971972
Sparse Core Ops, SparseCore 0:
  87.5 48.3 reduce-scatter.7
  140.5 33.9 all-gather.4
  189.2 48.0 reduce-scatter.11
  240.7 48.0 reduce-scatter.9
  294.4 33.9 all-gather.6
  390.2 150.2 all-reduce.3
  544.9 47.0 reduce-scatter.13
  605.2 48.0 reduce-scatter.15
